TPU v7x, 32 devices: a whole 2x2x4 slice. The times are simulated.
32 devices in a mesh: groups: 2 (over x), seq: 16 (over z, y, core).
Axes of the slice: x: 2, y: 2, z: 4, core: 2. Of those that a mesh axis runs over, the one named last changes fastest.
Arguments:
- queries: bfloat16 [64, 4, 8192], P(('groups', 'seq')), parts along dimension 0, may hold values from -128 to 128
- step_keys: bfloat16 [64, 4, 1024], P(('groups', 'seq')), parts along dimension 0, may hold values from -15 to 15
- step_values: bfloat16 [64, 4, 1024], P(('groups', 'seq')), parts along dimension 0, may hold values from -48 to 48
- sample_keys: bfloat16 [64, 1024, 1024], P(('groups', 'seq')), parts along dimension 0, may hold values from -6 to 6
- sample_values: bfloat16 [64, 1024, 1024], P(('groups', 'seq')), parts along dimension 0, may hold values from -48 to 48
- suffix_len: int32 [64], P(('groups', 'seq')), parts along dimension 0, may hold values from 128 to 1024
- prompt_id: int32 [64], P(('groups', 'seq')), parts along dimension 0, may hold values from 0 to 1, as said below
- document_keys: bfloat16 [4, 4096, 1024], P('groups', 'seq'), parts along dimension 0, may hold values from -6 to 6
- document_values: bfloat16 [4, 4096, 1024], P('groups', 'seq'), parts along dimension 0, may hold values from -48 to 48
Outputs:
- attended: bfloat16 [64, 4, 8192], P(('groups', 'seq')), parts along dimension 0
There are 2 independent parts, one for each index of `groups`. A program takes and returns all parts, laid end to end along the dimension named above; each array names one. Nothing has to cross between parts.
Inputs may be any that keep to these rules, and one draw needn't show every extreme that they name: `prompt_id`: each prompt id is held by exactly 16 samples.
All inputs are finite; a program needn't handle non-finite values.
Results may differ from a plain program's by a relative error of at most 0.0013.
Values may be sent and summed in bfloat16 or wider, within the bound.
A program may use at most 192 MiB of HBM per device.

v0:
```python
import jax
import jax.numpy as jnp
from jax import lax
from jax.sharding import PartitionSpec as P

QUERY_HEADS = 64
KEY_VALUE_HEADS = 8
HEAD_SIZE = 128


def shifted(block, axis, distance):
    devices = range(lax.axis_size(axis))
    route = [(i - distance, i) for i in devices if i - distance in devices]
    return lax.ppermute(block, axis, route)


def finish_merge(got_out, got_max, got_total, local_part):
    highest = jnp.maximum(jnp.max(got_max, axis=0), local_part[1])
    weights = jnp.exp(got_max - highest[None])
    local_weight = jnp.exp(local_part[1] - highest)
    numerator = (
        jnp.sum(got_out * weights[..., None], axis=0) + local_part[0] * local_weight[..., None]
    )
    denominator = jnp.sum(got_total * weights, axis=0) + local_part[2] * local_weight
    return (numerator, denominator)


def body(
    queries,
    step_keys,
    step_values,
    sample_keys,
    sample_values,
    suffix_len,
    prompt_id,
    document_keys,
    document_values,
):
    group_count = QUERY_HEADS // KEY_VALUE_HEADS
    scaling = HEAD_SIZE ** (-0.5)
    prompt_list = document_keys.shape[0]
    block_length = document_keys.shape[1]
    owned_rows = queries.shape[0]
    step_count = queries.shape[1]
    cache_length = sample_keys.shape[1]
    device_count = lax.axis_size("seq")
    owned_query = queries.reshape(owned_rows, step_count, KEY_VALUE_HEADS, group_count, HEAD_SIZE)
    cached_key_set = sample_keys.reshape(owned_rows, cache_length, KEY_VALUE_HEADS, HEAD_SIZE)
    cached_value_set = sample_values.reshape(owned_rows, cache_length, KEY_VALUE_HEADS, HEAD_SIZE)
    recent_keys = step_keys.reshape(owned_rows, step_count, KEY_VALUE_HEADS, HEAD_SIZE)
    recent_values = step_values.reshape(owned_rows, step_count, KEY_VALUE_HEADS, HEAD_SIZE)
    cache_scores = (
        jnp.einsum(
            "stgrd,skgd->stgrk", owned_query, cached_key_set, preferred_element_type=jnp.float32
        )
        * scaling
    )
    fresh_scores = (
        jnp.einsum(
            "stgrd,sugd->stgru", owned_query, recent_keys, preferred_element_type=jnp.float32
        )
        * scaling
    )
    cache_live = (jnp.arange(cache_length, dtype=jnp.int32)[None, :] < suffix_len[:, None])[
        :, None, None, None, :
    ]
    fresh_live = (jnp.arange(step_count)[None, :] <= jnp.arange(step_count)[:, None])[
        None, :, None, None, :
    ]
    local_max = jnp.maximum(
        jnp.max(jnp.where(cache_live, cache_scores, -jnp.inf), axis=-1),
        jnp.max(jnp.where(fresh_live, fresh_scores, -jnp.inf), axis=-1),
    )
    cache_exp = jnp.where(cache_live, jnp.exp(cache_scores - local_max[..., None]), 0.0)
    fresh_exp = jnp.where(fresh_live, jnp.exp(fresh_scores - local_max[..., None]), 0.0)
    local_total = jnp.sum(cache_exp, axis=-1) + jnp.sum(fresh_exp, axis=-1)
    local_out = jnp.einsum(
        "stgrk,skgd->stgrd",
        cache_exp.astype(jnp.bfloat16),
        cached_value_set,
        preferred_element_type=jnp.float32,
    ) + jnp.einsum(
        "stgru,sugd->stgrd",
        fresh_exp.astype(jnp.bfloat16),
        recent_values,
        preferred_element_type=jnp.float32,
    )
    local_part = (
        local_out.reshape(owned_rows, step_count, QUERY_HEADS, HEAD_SIZE),
        local_max.reshape(owned_rows, step_count, QUERY_HEADS),
        local_total.reshape(owned_rows, step_count, QUERY_HEADS),
    )
    my_head = lax.axis_index("seq") % KEY_VALUE_HEADS
    pair_rows = jnp.stack(
        (
            document_keys.reshape(prompt_list, block_length, KEY_VALUE_HEADS, HEAD_SIZE),
            document_values.reshape(prompt_list, block_length, KEY_VALUE_HEADS, HEAD_SIZE),
        ),
        0,
    )
    piece_list = [lax.dynamic_index_in_dim(pair_rows, my_head, 3, keepdims=False)]
    for offset in range(1, KEY_VALUE_HEADS):
        outgoing = lax.dynamic_index_in_dim(
            pair_rows, (my_head + offset) % KEY_VALUE_HEADS, 3, keepdims=False
        )
        forward = shifted(outgoing, "seq", offset)
        backward = shifted(outgoing, "seq", offset - KEY_VALUE_HEADS)
        piece_list.append(jnp.where(my_head >= offset, forward, backward))
    head_rows = jnp.stack(piece_list, 2)
    head_major = jnp.moveaxis(
        queries.reshape(owned_rows, step_count, KEY_VALUE_HEADS, group_count * HEAD_SIZE), 2, 0
    )
    position_groups = device_count // KEY_VALUE_HEADS
    tiled_rows = jnp.broadcast_to(head_major[None], (position_groups,) + head_major.shape).reshape(
        (device_count, owned_rows, step_count, group_count * HEAD_SIZE)
    )
    tiled_ids = jnp.broadcast_to(prompt_id[None], (device_count, owned_rows))
    head_queries, head_ids = (
        lax.all_to_all(tiled_rows, "seq", split_axis=0, concat_axis=0, tiled=True),
        lax.all_to_all(tiled_ids, "seq", split_axis=0, concat_axis=0, tiled=True),
    )
    samples = device_count * owned_rows
    prompt_count = samples // prompt_list
    head_queries = head_queries.reshape(samples, step_count, group_count, HEAD_SIZE)
    head_ids = head_ids.reshape(samples)
    rank_order = jnp.argsort(head_ids, stable=True)
    ordered_rows = head_queries[rank_order].reshape(
        prompt_list, prompt_count, step_count, group_count, HEAD_SIZE
    )
    scores = (
        jnp.einsum(
            "pntrd,pbkd->pbntrk", ordered_rows, head_rows[0], preferred_element_type=jnp.float32
        )
        * scaling
    )
    peak = jnp.max(scores, axis=-1)
    expo = jnp.exp(scores - peak[..., None])
    total = jnp.sum(expo, axis=-1)
    result = jnp.einsum(
        "pbntrk,pbkd->pbntrd",
        expo.astype(jnp.bfloat16),
        head_rows[1],
        preferred_element_type=jnp.float32,
    )
    top = jnp.max(peak, axis=1)
    block_weight = jnp.exp(peak - top[:, None])
    merged_out = jnp.sum(result * block_weight[..., None], axis=1)
    merged_total = jnp.sum(total * block_weight, axis=1)
    inverse = (
        jnp.zeros((samples,), jnp.int32).at[rank_order].set(jnp.arange(samples, dtype=jnp.int32))
    )
    part_out = merged_out.reshape(samples, step_count, group_count, HEAD_SIZE)[inverse]
    part_max = top.reshape(samples, step_count, group_count)[inverse]
    part_total = merged_total.reshape(samples, step_count, group_count)[inverse]
    got_out, got_max, got_total = (
        lax.all_to_all(
            part_out.reshape(device_count, owned_rows, step_count, group_count, HEAD_SIZE),
            "seq",
            split_axis=0,
            concat_axis=0,
            tiled=True,
        ),
        lax.all_to_all(
            part_max.reshape(device_count, owned_rows, step_count, group_count),
            "seq",
            split_axis=0,
            concat_axis=0,
            tiled=True,
        ),
        lax.all_to_all(
            part_total.reshape(device_count, owned_rows, step_count, group_count),
            "seq",
            split_axis=0,
            concat_axis=0,
            tiled=True,
        ),
    )
    got_out = jnp.moveaxis(
        got_out.reshape(
            position_groups, KEY_VALUE_HEADS, owned_rows, step_count, group_count, HEAD_SIZE
        ),
        1,
        3,
    )
    got_out = got_out.reshape(position_groups, owned_rows, step_count, QUERY_HEADS, HEAD_SIZE)
    got_max = jnp.moveaxis(
        got_max.reshape(position_groups, KEY_VALUE_HEADS, owned_rows, step_count, group_count), 1, 3
    )
    got_max = got_max.reshape(position_groups, owned_rows, step_count, QUERY_HEADS)
    got_total = jnp.moveaxis(
        got_total.reshape(position_groups, KEY_VALUE_HEADS, owned_rows, step_count, group_count),
        1,
        3,
    )
    got_total = got_total.reshape(position_groups, owned_rows, step_count, QUERY_HEADS)
    numerator, denominator = finish_merge(got_out, got_max, got_total, local_part)
    attended = numerator / denominator[..., None]
    return attended.reshape(owned_rows, step_count, QUERY_HEADS * HEAD_SIZE).astype(jnp.bfloat16)


def solution(mesh):
    return jax.shard_map(
        body,
        mesh=mesh,
        in_specs=(
            P(("groups", "seq"), None, None),
            P(("groups", "seq"), None, None),
            P(("groups", "seq"), None, None),
            P(("groups", "seq"), None, None),
            P(("groups", "seq"), None, None),
            P(("groups", "seq")),
            P(("groups", "seq")),
            P("groups", "seq", None),
            P("groups", "seq", None),
        ),
        out_specs=P(("groups", "seq"), None, None),
        check_vma=False,
    )
```

profile of v0, /device:TPU:0, one launch (start us, length us, event | category | flops | bytes accessed | tf_op | source)
XLA Modules:
  0.0 159.8 jit_solution(7076308821209347428)
XLA Ops:
  3.7 2.4 %collective-permute-start = (bf16[2,2,256,128]{3,2,1,0:T(8,128)(2,1)}, bf16[2,2,256,128]{3,2,1,0:T(8,128)(2,1)S(1)}, u32[]{:S(2)}, u32[]{:S(2)}) collective-permute-start(bf16[2,2,256,128]{3,2,1,0:T(8,128)(2,1)} %get-tuple-element.24), channel_id=1, source_target_pairs={{0,1},{1,2},{2,3},{3,4},{4,5},{5,6},{6,7},{7,8},{8,9},{9,10},{10,1... | collective-permute-start | bytes 786440 | tf_op jit(solution)/shard_map/ppermute | solution.py:14
  7.5 4.4 %collective-permute-start.2 = (bf16[2,2,256,128]{3,2,1,0:T(8,128)(2,1)}, bf16[2,2,256,128]{3,2,1,0:T(8,128)(2,1)S(1)}, u32[]{:S(2)}, u32[]{:S(2)}) collective-permute-start(bf16[2,2,256,128]{3,2,1,0:T(8,128)(2,1)} %get-tuple-element.23), channel_id=1, source_target_pairs={{0,2},{1,3},{2,4},{3,5},{4,6},{5,7},{6,8},{7,9},{8,10},{9,11},{10,... | collective-permute-start | bytes 786440 | tf_op jit(solution)/shard_map/ppermute | solution.py:14
  13.8 9.9 %all-to-all-start.1 = ((s32[16,1,2]{2,1,0:T(1,128)}), s32[16,1,2]{2,1,0:T(1,128)}, u32[]{:S(2)}, u32[]{:S(2)}) async-start(s32[16,1,2]{2,1,0:T(1,128)} %broadcast_in_dim.75), calls=%async_computation.1 | async-start | bytes 16384 | tf_op jit(solution)/shard_map/all_to_all | solution.py:120
  23.7 3.5 %collective-permute-start.4 = (bf16[2,2,256,128]{3,2,1,0:T(8,128)(2,1)}, bf16[2,2,256,128]{3,2,1,0:T(8,128)(2,1)S(1)}, u32[]{:S(2)}, u32[]{:S(2)}) collective-permute-start(bf16[2,2,256,128]{3,2,1,0:T(8,128)(2,1)} %get-tuple-element.22), channel_id=1, source_target_pairs={{0,3},{1,4},{2,5},{3,6},{4,7},{5,8},{6,9},{7,10},{8,11},{9,12},{10... | collective-permute-start | bytes 786440 | tf_op jit(solution)/shard_map/ppermute | solution.py:14
  29.4 3.3 %copy.238 = bf16[256,8,8,128]{3,2,1,0:T(8,128)(2,1)S(1)} copy(bf16[256,8,8,128]{3,1,2,0:T(8,128)(2,1)} %bitcast.164) | data formatting | bytes 8388608
  36.0 2.2 %bitcast_bitcast_fusion = bf16[2,1024,8,128,1]{3,2,1,0,4:T(8,128)(2,1)} fusion(bf16[2,1024,8,128]{3,2,1,0:T(8,128)(2,1)S(1)} %bitcast.163), kind=kLoop, calls=%fused_computation.11 | loop fusion | bytes 8388608 | tf_op jit(solution)/shard_map/reshape | solution.py:49
  39.5 2.2 %fusion.11 = (f32[2,4,8,8]{3,1,2,0:T(4,128)}, f32[2,8,1024,4,8]{2,4,3,1,0:T(8,128)S(1)}) fusion(pred[2,1024]{1,0:T(4,128)(4,1)S(1)} %iota_compare_fusion, bf16[2,4,8,8,128]{4,3,2,1,0:T(8,128)(2,1)S(1)} %reshape.209, bf16[2,1024,8,128,1]{3,2,1,0,4:T(8,128)(2,1)S(1)} %bitcast_bitcast_fusion.1), kind=kOutput, calls=%fused_computation.22 | convolution fusion | flops 135790080 | bytes 6426624 | tf_op jit(solution)/shard_map/stgrd,skgd->stgrk/dot_general | solution.py:53
  42.7 4.6 %all-to-all-start = ((bf16[16,2,4,1024]{3,2,1,0:T(4,128)(2,1)}), bf16[16,2,4,1024]{3,2,1,0:T(4,128)(2,1)S(1)}, u32[]{:S(2)}, u32[]{:S(2)}) async-start(bf16[16,2,4,1024]{3,2,1,0:T(4,128)(2,1)} %bitcast.19), calls=%async_computation | async-start | bytes 524288 | tf_op jit(solution)/shard_map/all_to_all | solution.py:119
  51.6 2.3 %sort.17 = (s32[32]{0:T(128)}, s32[32]{0:T(128)}) sort(s32[32]{0:T(128)} %reshape.200, s32[32]{0:T(128)} %iota.29), dimensions={0}, to_apply=%region_0.1 | sort | flops 160 | bytes 512 | tf_op jit(solution)/shard_map/jit(argsort)/sort | solution.py:126
  60.7 3.8 %collective-permute-start.6 = (bf16[2,2,256,128]{3,2,1,0:T(8,128)(2,1)}, bf16[2,2,256,128]{3,2,1,0:T(8,128)(2,1)S(1)}, u32[]{:S(2)}, u32[]{:S(2)}) collective-permute-start(bf16[2,2,256,128]{3,2,1,0:T(8,128)(2,1)} %get-tuple-element.21), channel_id=1, source_target_pairs={{0,4},{1,5},{2,6},{3,7},{4,8},{5,9},{6,10},{7,11},{8,12},{9,13},{1... | collective-permute-start | bytes 786440 | tf_op jit(solution)/shard_map/ppermute | solution.py:14
  67.6 3.7 %collective-permute-start.8 = (bf16[2,2,256,128]{3,2,1,0:T(8,128)(2,1)}, bf16[2,2,256,128]{3,2,1,0:T(8,128)(2,1)S(1)}, u32[]{:S(2)}, u32[]{:S(2)}) collective-permute-start(bf16[2,2,256,128]{3,2,1,0:T(8,128)(2,1)} %get-tuple-element.20), channel_id=1, source_target_pairs={{0,5},{1,6},{2,7},{3,8},{4,9},{5,10},{6,11},{7,12},{8,13},{9,14},{... | collective-permute-start | bytes 786440 | tf_op jit(solution)/shard_map/ppermute | solution.py:14
  73.3 8.2 %collective-permute-start.10 = (bf16[2,2,256,128]{3,2,1,0:T(8,128)(2,1)}, bf16[2,2,256,128]{3,2,1,0:T(8,128)(2,1)S(1)}, u32[]{:S(2)}, u32[]{:S(2)}) collective-permute-start(bf16[2,2,256,128]{3,2,1,0:T(8,128)(2,1)} %get-tuple-element.19), channel_id=1, source_target_pairs={{0,6},{1,7},{2,8},{3,9},{4,10},{5,11},{6,12},{7,13},{8,14},{9,15},... | collective-permute-start | bytes 786440 | tf_op jit(solution)/shard_map/ppermute | solution.py:14
  83.7 2.8 %collective-permute-start.12 = (bf16[2,2,256,128]{3,2,1,0:T(8,128)(2,1)S(1)}, bf16[2,2,256,128]{3,2,1,0:T(8,128)(2,1)S(1)}, u32[]{:S(2)}, u32[]{:S(2)}) collective-permute-start(bf16[2,2,256,128]{3,2,1,0:T(8,128)(2,1)S(1)} %copy-done.4), channel_id=1, source_target_pairs={{0,7},{1,8},{2,9},{3,10},{4,11},{5,12},{6,13},{7,14},{8,15},{16,23... | collective-permute-start | bytes 786440 | tf_op jit(solution)/shard_map/ppermute | solution.py:14
  90.5 2.1 %collective-permute-done.11 = bf16[2,2,256,128]{3,2,1,0:T(8,128)(2,1)S(1)} collective-permute-done((bf16[2,2,256,128]{3,2,1,0:T(8,128)(2,1)S(1)}, bf16[2,2,256,128]{3,2,1,0:T(8,128)(2,1)S(1)}, u32[]{:S(2)}, u32[]{:S(2)}) %collective-permute-start.11) | collective-permute-done | bytes 262176 | tf_op jit(solution)/shard_map/ppermute | solution.py:14
  93.4 2.6 %collective-permute-done.12 = bf16[2,2,256,128]{3,2,1,0:T(8,128)(2,1)S(1)} collective-permute-done((bf16[2,2,256,128]{3,2,1,0:T(8,128)(2,1)S(1)}, bf16[2,2,256,128]{3,2,1,0:T(8,128)(2,1)S(1)}, u32[]{:S(2)}, u32[]{:S(2)}) %collective-permute-start.12) | collective-permute-done | bytes 262176 | tf_op jit(solution)/shard_map/ppermute | solution.py:14
  97.6 2.6 %bitcast_reduce_fusion.1 = (f32[2,8,16,4,8]{2,4,3,1,0:T(8,128)S(1)}, f32[2,8,256,16,4,8]{2,3,5,4,1,0:T(8,128)S(1)}) fusion(bf16[2,16,4,8,128,1]{4,3,2,1,0,5:T(8,128)(2,1)S(1)} %bitcast.169, bf16[2,2,8,256,128]{4,3,2,1,0:T(8,128)(2,1)} %bitcast_dynamic-update-slice_fusion), kind=kOutput, calls=%fused_computation.7 | convolution fusion | flops 541057024 | bytes 9732096 | tf_op jit(solution)/shard_map/pntrd,pbkd->pbntrk/dot_general | solution.py:131
  100.2 4.8 %fusion.1 = (f32[2,8,16,4,8]{2,4,3,1,0:T(8,128)S(1)}, f32[2,16,4,8]{1,3,2,0:T(8,128)S(1)}, bf16[2,8,16,4,8,256]{5,2,4,3,1,0:T(8,128)(2,1)}) fusion(f32[2,8,256,16,4,8]{2,3,5,4,1,0:T(8,128)S(1)} %get-tuple-element.27, f32[2,8,16,4,8]{2,4,3,1,0:T(8,128)S(1)} %get-tuple-element.26), kind=kLoop, calls=%fused_computation.9 | loop fusion | flops 10476544 | bytes 12652544 | tf_op jit(solution)/shard_map/reduce_sum | solution.py:138
  106.5 14.3 %all-to-all-start.3 = ((f32[16,2,4,8]{3,1,2,0:T(2,128)}), f32[16,2,4,8]{3,1,2,0:T(2,128)S(1)}, u32[]{:S(2)}, u32[]{:S(2)}) async-start(f32[16,2,4,8]{3,1,2,0:T(2,128)} %copy.193), calls=%async_computation.3 | async-start | bytes 131072 | tf_op jit(solution)/shard_map/all_to_all | solution.py:163
  121.1 4.2 %multiply_reduce_fusion = f32[2,16,4,8,128]{4,3,2,1,0:T(8,128)S(1)} fusion(bf16[2,8,16,4,8,256]{5,2,4,3,1,0:T(8,128)(2,1)} %get-tuple-element.17, f32[2,8,16,4,8]{4,3,2,1,0:T(4,128)S(1)} %copy.189, bf16[2,2,8,256,128]{4,3,2,1,0:T(8,128)(2,1)} %bitcast_dynamic-update-slice_fusion), kind=kOutput, calls=%fused_computation.19 | convolution fusion | flops 538836992 | bytes 5799936 | tf_op jit(solution)/shard_map/pbntrk,pbkd->pbntrd/dot_general | solution.py:139
  128.3 5.7 %all-to-all-start.4 = ((f32[16,2,4,8]{3,1,2,0:T(2,128)}), f32[16,2,4,8]{3,1,2,0:T(2,128)S(1)}, u32[]{:S(2)}, u32[]{:S(2)}) async-start(f32[16,2,4,8]{3,1,2,0:T(2,128)} %copy.213), calls=%async_computation.4 | async-start | bytes 131072 | tf_op jit(solution)/shard_map/all_to_all | solution.py:170
  134.1 6.8 %all-to-all-done.4 = f32[16,2,4,8]{3,1,2,0:T(2,128)S(1)} async-done(((f32[16,2,4,8]{3,1,2,0:T(2,128)}), f32[16,2,4,8]{3,1,2,0:T(2,128)S(1)}, u32[]{:S(2)}, u32[]{:S(2)}) %all-to-all-start.4) | async-done | bytes 4128 | tf_op jit(solution)/shard_map/all_to_all | solution.py:170
  140.9 3.6 %all-to-all-start.2 = ((f32[16,2,4,8,128]{4,3,2,1,0:T(8,128)}), f32[16,2,4,8,128]{4,3,2,1,0:T(8,128)S(1)}, u32[]{:S(2)}, u32[]{:S(2)}) async-start(f32[16,2,4,8,128]{4,3,2,1,0:T(8,128)} %bitcast.27), calls=%async_computation.2 | async-start | bytes 1048576 | tf_op jit(solution)/shard_map/all_to_all | solution.py:156
  146.0 3.7 %fusion.3 = f32[2,8,4,8,128]{4,3,2,1,0:T(8,128)S(1)} fusion(bf16[2,1024,8,128,1]{3,2,1,0,4:T(8,128)(2,1)} %bitcast_bitcast_fusion, f32[2,8,1024,4,8]{2,4,3,1,0:T(8,128)S(1)} %get-tuple-element.31, f32[2,4,8,8]{3,1,2,0:T(4,128)S(1)} %copy.205, pred[2,1024]{1,0:T(4,128)(4,1)S(1)} %copy-done.9), kind=kOutput, calls=%fused_computation.13 | convolution fusion | flops 136314880 | bytes 6557696 | tf_op jit(solution)/shard_map/stgrk,skgd->stgrd/dot_general | solution.py:77
  150.5 8.2 %all-to-all-done.2 = f32[16,2,4,8,128]{4,3,2,1,0:T(8,128)S(1)} async-done(((f32[16,2,4,8,128]{4,3,2,1,0:T(8,128)}), f32[16,2,4,8,128]{4,3,2,1,0:T(8,128)S(1)}, u32[]{:S(2)}, u32[]{:S(2)}) %all-to-all-start.2) | async-done | bytes 524320 | tf_op jit(solution)/shard_map/all_to_all | solution.py:156
  (121 shorter events, 47.3 us)
Async XLA Ops:
  0.0 149.8 %copy-start = (bf16[2,4,1024]{2,1,0:T(4,128)(2,1)S(1)}, bf16[2,4,1024]{2,1,0:T(4,128)(2,1)}, u32[]{:S(2)}) copy-start(bf16[2,4,1024]{2,1,0:T(4,128)(2,1)} %param.11) | copy-start | bytes 49156
  2.4 25.3 %copy-start.3 = (bf16[2,4,8192]{2,1,0:T(4,128)(2,1)S(1)}, bf16[2,4,8192]{2,1,0:T(4,128)(2,1)}, u32[]{:S(2)}) copy-start(bf16[2,4,8192]{2,1,0:T(4,128)(2,1)} %param.9) | copy-start | bytes 393220
  3.7 55.7 %collective-permute-start = (bf16[2,2,256,128]{3,2,1,0:T(8,128)(2,1)}, bf16[2,2,256,128]{3,2,1,0:T(8,128)(2,1)S(1)}, u32[]{:S(2)}, u32[]{:S(2)}) collective-permute-start(bf16[2,2,256,128]{3,2,1,0:T(8,128)(2,1)} %get-tuple-element.24), channel_id=1, source_target_pairs={{0,1},{1,2},{2,3},{3,4},{4,5},{5,6},{6,7},{7,8},{8,9},{9,10},{10,1... | collective-permute-start | bytes 786440 | tf_op jit(solution)/shard_map/ppermute | solution.py:14
  6.2 54.5 %collective-permute-start.1 = (bf16[2,2,256,128]{3,2,1,0:T(8,128)(2,1)}, bf16[2,2,256,128]{3,2,1,0:T(8,128)(2,1)}, u32[]{:S(2)}, u32[]{:S(2)}) collective-permute-start(bf16[2,2,256,128]{3,2,1,0:T(8,128)(2,1)} %get-tuple-element.24), channel_id=1, source_target_pairs={{7,0},{8,1},{9,2},{10,3},{11,4},{12,5},{13,6},{14,7},{15,8},{23,16... | collective-permute-start | bytes 786440 | tf_op jit(solution)/shard_map/ppermute | solution.py:14
  7.5 58.8 %collective-permute-start.2 = (bf16[2,2,256,128]{3,2,1,0:T(8,128)(2,1)}, bf16[2,2,256,128]{3,2,1,0:T(8,128)(2,1)S(1)}, u32[]{:S(2)}, u32[]{:S(2)}) collective-permute-start(bf16[2,2,256,128]{3,2,1,0:T(8,128)(2,1)} %get-tuple-element.23), channel_id=1, source_target_pairs={{0,2},{1,3},{2,4},{3,5},{4,6},{5,7},{6,8},{7,9},{8,10},{9,11},{10,... | collective-permute-start | bytes 786440 | tf_op jit(solution)/shard_map/ppermute | solution.py:14
  11.9 55.7 %collective-permute-start.3 = (bf16[2,2,256,128]{3,2,1,0:T(8,128)(2,1)}, bf16[2,2,256,128]{3,2,1,0:T(8,128)(2,1)S(1)}, u32[]{:S(2)}, u32[]{:S(2)}) collective-permute-start(bf16[2,2,256,128]{3,2,1,0:T(8,128)(2,1)} %get-tuple-element.23), channel_id=1, source_target_pairs={{6,0},{7,1},{8,2},{9,3},{10,4},{11,5},{12,6},{13,7},{14,8},{15,9},... | collective-permute-start | bytes 786440 | tf_op jit(solution)/shard_map/ppermute | solution.py:14
  13.8 28.0 %all-to-all-start.1 = ((s32[16,1,2]{2,1,0:T(1,128)}), s32[16,1,2]{2,1,0:T(1,128)}, u32[]{:S(2)}, u32[]{:S(2)}) async-start(s32[16,1,2]{2,1,0:T(1,128)} %broadcast_in_dim.75), calls=%async_computation.1 | async-start | bytes 16384 | tf_op jit(solution)/shard_map/all_to_all | solution.py:120
  23.7 48.4 %collective-permute-start.4 = (bf16[2,2,256,128]{3,2,1,0:T(8,128)(2,1)}, bf16[2,2,256,128]{3,2,1,0:T(8,128)(2,1)S(1)}, u32[]{:S(2)}, u32[]{:S(2)}) collective-permute-start(bf16[2,2,256,128]{3,2,1,0:T(8,128)(2,1)} %get-tuple-element.22), channel_id=1, source_target_pairs={{0,3},{1,4},{2,5},{3,6},{4,7},{5,8},{6,9},{7,10},{8,11},{9,12},{10... | collective-permute-start | bytes 786440 | tf_op jit(solution)/shard_map/ppermute | solution.py:14
  42.7 54.1 %all-to-all-start = ((bf16[16,2,4,1024]{3,2,1,0:T(4,128)(2,1)}), bf16[16,2,4,1024]{3,2,1,0:T(4,128)(2,1)S(1)}, u32[]{:S(2)}, u32[]{:S(2)}) async-start(bf16[16,2,4,1024]{3,2,1,0:T(4,128)(2,1)} %bitcast.19), calls=%async_computation | async-start | bytes 524288 | tf_op jit(solution)/shard_map/all_to_all | solution.py:119
  56.9 25.5 %copy-start.5 = (bf16[2,2,256,128]{3,2,1,0:T(8,128)(2,1)S(1)}, bf16[2,2,256,128]{3,2,1,0:T(8,128)(2,1)}, u32[]{:S(2)}) copy-start(bf16[2,2,256,128]{3,2,1,0:T(8,128)(2,1)} %get-tuple-element.19) | copy-start | bytes 786436
  56.9 26.8 %copy-start.4 = (bf16[2,2,256,128]{3,2,1,0:T(8,128)(2,1)S(1)}, bf16[2,2,256,128]{3,2,1,0:T(8,128)(2,1)}, u32[]{:S(2)}) copy-start(bf16[2,2,256,128]{3,2,1,0:T(8,128)(2,1)} %get-tuple-element.18) | copy-start | bytes 786436
  59.4 13.9 %collective-permute-start.5 = (bf16[2,2,256,128]{3,2,1,0:T(8,128)(2,1)}, bf16[2,2,256,128]{3,2,1,0:T(8,128)(2,1)S(1)}, u32[]{:S(2)}, u32[]{:S(2)}) collective-permute-start(bf16[2,2,256,128]{3,2,1,0:T(8,128)(2,1)} %get-tuple-element.22), channel_id=1, source_target_pairs={{5,0},{6,1},{7,2},{8,3},{9,4},{10,5},{11,6},{12,7},{13,8},{14,9},{... | collective-permute-start | bytes 786440 | tf_op jit(solution)/shard_map/ppermute | solution.py:14
  60.7 21.6 %collective-permute-start.6 = (bf16[2,2,256,128]{3,2,1,0:T(8,128)(2,1)}, bf16[2,2,256,128]{3,2,1,0:T(8,128)(2,1)S(1)}, u32[]{:S(2)}, u32[]{:S(2)}) collective-permute-start(bf16[2,2,256,128]{3,2,1,0:T(8,128)(2,1)} %get-tuple-element.21), channel_id=1, source_target_pairs={{0,4},{1,5},{2,6},{3,7},{4,8},{5,9},{6,10},{7,11},{8,12},{9,13},{1... | collective-permute-start | bytes 786440 | tf_op jit(solution)/shard_map/ppermute | solution.py:14
  66.3 17.3 %collective-permute-start.7 = (bf16[2,2,256,128]{3,2,1,0:T(8,128)(2,1)}, bf16[2,2,256,128]{3,2,1,0:T(8,128)(2,1)S(1)}, u32[]{:S(2)}, u32[]{:S(2)}) collective-permute-start(bf16[2,2,256,128]{3,2,1,0:T(8,128)(2,1)} %get-tuple-element.21), channel_id=1, source_target_pairs={{4,0},{5,1},{6,2},{7,3},{8,4},{9,5},{10,6},{11,7},{12,8},{13,9},{1... | collective-permute-start | bytes 786440 | tf_op jit(solution)/shard_map/ppermute | solution.py:14
  67.6 19.6 %collective-permute-start.8 = (bf16[2,2,256,128]{3,2,1,0:T(8,128)(2,1)}, bf16[2,2,256,128]{3,2,1,0:T(8,128)(2,1)S(1)}, u32[]{:S(2)}, u32[]{:S(2)}) collective-permute-start(bf16[2,2,256,128]{3,2,1,0:T(8,128)(2,1)} %get-tuple-element.20), channel_id=1, source_target_pairs={{0,5},{1,6},{2,7},{3,8},{4,9},{5,10},{6,11},{7,12},{8,13},{9,14},{... | collective-permute-start | bytes 786440 | tf_op jit(solution)/shard_map/ppermute | solution.py:14
  72.0 16.7 %collective-permute-start.9 = (bf16[2,2,256,128]{3,2,1,0:T(8,128)(2,1)}, bf16[2,2,256,128]{3,2,1,0:T(8,128)(2,1)S(1)}, u32[]{:S(2)}, u32[]{:S(2)}) collective-permute-start(bf16[2,2,256,128]{3,2,1,0:T(8,128)(2,1)} %get-tuple-element.20), channel_id=1, source_target_pairs={{3,0},{4,1},{5,2},{6,3},{7,4},{8,5},{9,6},{10,7},{11,8},{12,9},{13... | collective-permute-start | bytes 786440 | tf_op jit(solution)/shard_map/ppermute | solution.py:14
  73.3 17.1 %collective-permute-start.10 = (bf16[2,2,256,128]{3,2,1,0:T(8,128)(2,1)}, bf16[2,2,256,128]{3,2,1,0:T(8,128)(2,1)S(1)}, u32[]{:S(2)}, u32[]{:S(2)}) collective-permute-start(bf16[2,2,256,128]{3,2,1,0:T(8,128)(2,1)} %get-tuple-element.19), channel_id=1, source_target_pairs={{0,6},{1,7},{2,8},{3,9},{4,10},{5,11},{6,12},{7,13},{8,14},{9,15},... | collective-permute-start | bytes 786440 | tf_op jit(solution)/shard_map/ppermute | solution.py:14
  82.3 10.2 %collective-permute-start.11 = (bf16[2,2,256,128]{3,2,1,0:T(8,128)(2,1)S(1)}, bf16[2,2,256,128]{3,2,1,0:T(8,128)(2,1)S(1)}, u32[]{:S(2)}, u32[]{:S(2)}) collective-permute-start(bf16[2,2,256,128]{3,2,1,0:T(8,128)(2,1)S(1)} %copy-done.5), channel_id=1, source_target_pairs={{2,0},{3,1},{4,2},{5,3},{6,4},{7,5},{8,6},{9,7},{10,8},{11,9},{12,... | collective-permute-start | bytes 786440 | tf_op jit(solution)/shard_map/ppermute | solution.py:14
  83.7 12.3 %collective-permute-start.12 = (bf16[2,2,256,128]{3,2,1,0:T(8,128)(2,1)S(1)}, bf16[2,2,256,128]{3,2,1,0:T(8,128)(2,1)S(1)}, u32[]{:S(2)}, u32[]{:S(2)}) collective-permute-start(bf16[2,2,256,128]{3,2,1,0:T(8,128)(2,1)S(1)} %copy-done.4), channel_id=1, source_target_pairs={{0,7},{1,8},{2,9},{3,10},{4,11},{5,12},{6,13},{7,14},{8,15},{16,23... | collective-permute-start | bytes 786440 | tf_op jit(solution)/shard_map/ppermute | solution.py:14
  87.2 8.8 %collective-permute-start.13 = (bf16[2,2,256,128]{3,2,1,0:T(8,128)(2,1)S(1)}, bf16[2,2,256,128]{3,2,1,0:T(8,128)(2,1)S(1)}, u32[]{:S(2)}, u32[]{:S(2)}) collective-permute-start(bf16[2,2,256,128]{3,2,1,0:T(8,128)(2,1)S(1)} %copy-done.4), channel_id=1, source_target_pairs={{1,0},{2,1},{3,2},{4,3},{5,4},{6,5},{7,6},{8,7},{9,8},{10,9},{11,1... | collective-permute-start | bytes 786440 | tf_op jit(solution)/shard_map/ppermute | solution.py:14
  106.5 21.8 %all-to-all-start.3 = ((f32[16,2,4,8]{3,1,2,0:T(2,128)}), f32[16,2,4,8]{3,1,2,0:T(2,128)S(1)}, u32[]{:S(2)}, u32[]{:S(2)}) async-start(f32[16,2,4,8]{3,1,2,0:T(2,128)} %copy.193), calls=%async_computation.3 | async-start | bytes 131072 | tf_op jit(solution)/shard_map/all_to_all | solution.py:163
  125.3 19.3 %copy-start.9 = (pred[2,1024]{1,0:T(4,128)(4,1)S(1)}, pred[2,1024]{1,0:T(4,128)(4,1)}, u32[]{:S(2)}) copy-start(pred[2,1024]{1,0:T(4,128)(4,1)} %copy-done.8) | copy-start | bytes 6148
  128.3 12.6 %all-to-all-start.4 = ((f32[16,2,4,8]{3,1,2,0:T(2,128)}), f32[16,2,4,8]{3,1,2,0:T(2,128)S(1)}, u32[]{:S(2)}, u32[]{:S(2)}) async-start(f32[16,2,4,8]{3,1,2,0:T(2,128)} %copy.213), calls=%async_computation.4 | async-start | bytes 131072 | tf_op jit(solution)/shard_map/all_to_all | solution.py:170
  140.9 17.8 %all-to-all-start.2 = ((f32[16,2,4,8,128]{4,3,2,1,0:T(8,128)}), f32[16,2,4,8,128]{4,3,2,1,0:T(8,128)S(1)}, u32[]{:S(2)}, u32[]{:S(2)}) async-start(f32[16,2,4,8,128]{4,3,2,1,0:T(8,128)} %bitcast.27), calls=%async_computation.2 | async-start | bytes 1048576 | tf_op jit(solution)/shard_map/all_to_all | solution.py:156
  (9 other events, 72.2 us)
where the time goes:
time: 161 us; the launch traced here: 160 us
  starting transfers between devices  76.1 us (47%)
  local copies, waits for them, and re-layouts  25.8 us (16%)
  other arithmetic  22.3 us (14%)
  waiting for transfers between devices  20.7 us (13%)
  matrix products  14.3 us (9%)
    ppermute x14, starting transfers between devices, shifted(): return lax.ppermute(block, axis, route)  38 us
    all_to_all x1, starting transfers between devices, body(): lax.all_to_all(part_max.reshape(device_count, owned_rows, step_count, gro...  14.3 us
    all_to_all x1, starting transfers between devices, body(): lax.all_to_all(tiled_ids, 'seq', split_axis=0, concat_axis=0, tiled=True)  9.87 us
    unnamed x34, local copies, waits for them, and re-layouts  9.13 us
    all_to_all x1, waiting for transfers between devices, body(): lax.all_to_all(part_out.reshape(device_count, owned_rows, step_count, gro...  8.22 us
    all_to_all x1, waiting for transfers between devices, body(): lax.all_to_all(part_total.reshape(device_count, owned_rows, step_count, g...  6.76 us
    ppermute x14, waiting for transfers between devices, shifted(): return lax.ppermute(block, axis, route)  5.74 us
    all_to_all x1, starting transfers between devices, body(): lax.all_to_all(part_total.reshape(device_count, owned_rows, step_count, g...  5.69 us
  transfers between devices with their start and end apart: 19, of which 5 were waited for; matrix products, arithmetic and copies ran while one was open for 29% of the time, Pallas kernels for 0%

commit v1 on v0

v1 whole, which is shorter than its diff:
```python
import functools

import jax
import jax.numpy as jnp
from jax import lax
from jax.experimental import pallas as pl
from jax.experimental.pallas import tpu as pltpu
from jax.sharding import PartitionSpec as P

QUERY_HEADS = 64
KEY_VALUE_HEADS = 8
HEAD_SIZE = 128
LOG2E = 1.4426950408889634
ID_ROWS = 16
STAT_ROWS = 8
MESH = pl.DeviceIdType.MESH
NT = (((1,), (1,)), ((), ()))
NN = (((1,), (0,)), ((), ()))


def member(head, offset):
    result = 0
    for bit in range(3):
        weight = 1 << bit
        own = lax.rem(head // weight, 2)
        result = result + weight * (1 - own if offset & weight else own)
    return result


def kernel(
    n,
    len_ref,
    query_ref,
    step_key_ref,
    step_value_ref,
    sample_keys,
    sample_values,
    document_keys,
    document_values,
    out_ref,
    key_buf,
    value_buf,
    head_keys,
    head_values,
    query_buf,
    query_cat,
    id_buf,
    acc,
    acc_max,
    acc_total,
    send_buf,
    got_buf,
    own_out,
    own_max,
    own_total,
    local_sem,
    query_send,
    query_recv,
    pair_send,
    pair_recv,
    part_send,
    part_recv,
):
    me = lax.axis_index("seq")
    my_head = lax.rem(me, KEY_VALUE_HEADS)
    my_base = me - my_head
    samples, cache = sample_keys.shape[0], sample_keys.shape[1]
    steps = step_key_ref.shape[1]
    rows = query_ref.shape[2] - ID_ROWS
    owner_rows = samples * rows
    prompts = document_keys.shape[0]
    padded = key_buf.shape[1]
    factor = (HEAD_SIZE ** (-0.5)) * LOG2E

    def columns(head):
        return pl.ds(pl.multiple_of(head * HEAD_SIZE, HEAD_SIZE), HEAD_SIZE)

    local = [
        pltpu.make_async_copy(
            sample_keys, key_buf.at[:, pl.ds(0, cache), :], local_sem.at[0]
        ),
        pltpu.make_async_copy(
            sample_values, value_buf.at[:, pl.ds(0, cache), :], local_sem.at[1]
        ),
        pltpu.make_async_copy(
            document_keys.at[:, :, columns(my_head)], head_keys.at[0], local_sem.at[2]
        ),
        pltpu.make_async_copy(
            document_values.at[:, :, columns(my_head)], head_values.at[0], local_sem.at[3]
        ),
    ]
    for copy in local:
        copy.start()

    barrier = pltpu.get_barrier_semaphore()

    def greet(step, carry):
        other = lax.rem(me + step, n)
        pl.semaphore_signal(barrier, inc=1, device_id={"seq": other}, device_id_type=MESH)
        return carry

    lax.fori_loop(1, n, greet, 0)
    pl.semaphore_wait(barrier, n - 1)

    def send_query(step, carry):
        other = lax.rem(me + step, n)
        pltpu.make_async_remote_copy(
            src_ref=query_ref.at[lax.rem(other, KEY_VALUE_HEADS)],
            dst_ref=query_buf.at[me],
            send_sem=query_send,
            recv_sem=query_recv,
            device_id={"seq": other},
            device_id_type=MESH,
        ).start()
        return carry

    lax.fori_loop(1, n, send_query, 0)

    pairs = {}
    for offset in (6, 7, 4, 5, 2, 3, 1):
        head = member(my_head, offset)
        for kind, (source, target) in enumerate(
            ((document_keys, head_keys), (document_values, head_values))
        ):
            copy = pltpu.make_async_remote_copy(
                src_ref=source.at[:, :, columns(head)],
                dst_ref=target.at[offset],
                send_sem=pair_send.at[kind, offset],
                recv_sem=pair_recv.at[kind, offset],
                device_id={"seq": my_base + head},
                device_id_type=MESH,
            )
            copy.start()
            pairs[kind, offset] = copy

    query_buf[me] = query_ref[my_head]
    for s in range(samples):
        key_buf[s, pl.ds(cache, padded - cache), :] = jnp.zeros(
            (padded - cache, key_buf.shape[2]), key_buf.dtype
        )
        value_buf[s, pl.ds(cache, padded - cache), :] = jnp.zeros(
            (padded - cache, value_buf.shape[2]), value_buf.dtype
        )
        key_buf[s, pl.ds(cache, steps), :] = step_key_ref[s]
        value_buf[s, pl.ds(cache, steps), :] = step_value_ref[s]
    for copy in local:
        copy.wait()

    slot = lax.broadcasted_iota(jnp.int32, (rows, padded), 1)
    now = lax.broadcasted_iota(jnp.int32, (rows, padded), 0) // (rows // steps)
    fresh = (slot >= cache) & (slot - cache <= now)

    def suffix_head(head, carry):
        for s in range(samples):
            query = query_ref[head, s, pl.ds(0, rows), :]
            scores = lax.dot_general(
                query, key_buf[s, :, columns(head)], NT, preferred_element_type=jnp.float32
            )
            live = (slot < len_ref[s]) | fresh
            scores = jnp.where(live, scores, -jnp.inf)
            peak = jnp.max(scores, axis=1, keepdims=True)
            expo = jnp.exp2((scores - peak) * factor)
            part = pl.ds(s * rows, rows)
            own_max[head, part, :] = peak
            own_total[head, part, :] = jnp.sum(expo, axis=1, keepdims=True)
            own_out[head, part, :] = lax.dot_general(
                expo.astype(jnp.bfloat16),
                value_buf[s, :, columns(head)],
                NN,
                preferred_element_type=jnp.float32,
            )
        return carry

    lax.fori_loop(0, KEY_VALUE_HEADS, suffix_head, 0)

    others = query_buf.at[pl.ds(0, n - 1)]
    pltpu.make_async_copy(others, others, query_recv).wait()

    def place(source, carry):
        for s in range(samples):
            query = query_buf[source, s, pl.ds(0, rows), :].astype(jnp.float32)
            mark = query_buf[source, s, pl.ds(rows, ID_ROWS), :].astype(jnp.float32)
            mark = jnp.concatenate([mark] * (rows // ID_ROWS), axis=0)
            part = pl.ds(pl.multiple_of(source * owner_rows + s * rows, rows), rows)
            for p in range(prompts):
                query_cat[part, pl.ds(p * HEAD_SIZE, HEAD_SIZE)] = jnp.where(
                    mark == p, query, 0.0
                ).astype(jnp.bfloat16)
            id_buf[part, :] = mark
            acc[part, :] = jnp.zeros((rows, HEAD_SIZE), jnp.float32)
            acc_max[part, :] = jnp.full((rows, 1), -1e30, jnp.float32)
            acc_total[part, :] = jnp.zeros((rows, 1), jnp.float32)
        return carry

    lax.fori_loop(0, n, place, 0)

    owners = 4 if n % 4 == 0 else 1
    chunk = owners * owner_rows

    def attend(offset, index):
        part = pl.ds(pl.multiple_of(index * chunk, chunk), chunk)
        keys = jnp.concatenate([head_keys[offset, p] for p in range(prompts)], axis=1)
        values = jnp.concatenate([head_values[offset, p] for p in range(prompts)], axis=1)
        scores = lax.dot_general(
            query_cat[part, :], keys, NT, preferred_element_type=jnp.float32
        )
        peak = jnp.max(scores, axis=1, keepdims=True)
        expo = jnp.exp2((scores - peak) * factor)
        total = jnp.sum(expo, axis=1, keepdims=True)
        both = lax.dot_general(
            expo.astype(jnp.bfloat16), values, NN, preferred_element_type=jnp.float32
        )
        mark = id_buf[part, :]
        result = both[:, :HEAD_SIZE]
        for p in range(1, prompts):
            result = jnp.where(
                mark == p, both[:, p * HEAD_SIZE : (p + 1) * HEAD_SIZE], result
            )
        before = acc_max[part, :]
        top = jnp.maximum(before, peak)
        old = jnp.exp2((before - top) * factor)
        new = jnp.exp2((peak - top) * factor)
        return part, acc[part, :] * old + result * new, top, acc_total[part, :] * old + total * new

    def keep(offset, index):
        part, merged, top, total = attend(offset, index)
        acc[part, :] = merged
        acc_max[part, :] = top
        acc_total[part, :] = total

    def over_block(offset, carry):
        lax.fori_loop(0, n // owners, lambda i, c: (keep(offset, i), c)[1], 0)
        return carry

    over_block(0, 0)
    last = KEY_VALUE_HEADS - 1
    for offset in range(1, last):
        pairs[0, offset].wait_recv()
        pairs[1, offset].wait_recv()
        over_block(offset, 0)
    pairs[0, last].wait_recv()
    pairs[1, last].wait_recv()

    diagonal = lax.broadcasted_iota(jnp.int32, (owner_rows, HEAD_SIZE), 0) == (
        lax.broadcasted_iota(jnp.int32, (owner_rows, HEAD_SIZE), 1)
    )
    stat_row = lax.broadcasted_iota(jnp.int32, (STAT_ROWS, HEAD_SIZE), 0)

    def finish(index, carry):
        _, merged, top, total = attend(last, index)
        for j in range(owners):
            owner = index * owners + j
            cut = slice(j * owner_rows, (j + 1) * owner_rows)
            send_buf[owner, pl.ds(0, owner_rows), :] = merged[cut]
            peak_row = jnp.sum(jnp.where(diagonal, top[cut], 0.0), axis=0, keepdims=True)
            total_row = jnp.sum(jnp.where(diagonal, total[cut], 0.0), axis=0, keepdims=True)
            send_buf[owner, pl.ds(owner_rows, STAT_ROWS), :] = jnp.where(
                stat_row == 0, peak_row, jnp.where(stat_row == 1, total_row, 0.0)
            )

            @pl.when(owner != me)
            def _():
                pltpu.make_async_remote_copy(
                    src_ref=send_buf.at[owner],
                    dst_ref=got_buf.at[me],
                    send_sem=part_send,
                    recv_sem=part_recv,
                    device_id={"seq": owner},
                    device_id_type=MESH,
                ).start()

        return carry

    lax.fori_loop(0, n // owners, finish, 0)
    got_buf[me] = send_buf[me]
    others = got_buf.at[pl.ds(0, n - 1)]
    pltpu.make_async_copy(others, others, part_recv).wait()

    def merge(head, carry):
        top = own_max[head]
        parts = []
        for group in range(n // KEY_VALUE_HEADS):
            source = group * KEY_VALUE_HEADS + head
            stats = got_buf[source, pl.ds(owner_rows, STAT_ROWS), :]
            peak = jnp.sum(jnp.where(diagonal, stats[0:1], 0.0), axis=1, keepdims=True)
            total = jnp.sum(jnp.where(diagonal, stats[1:2], 0.0), axis=1, keepdims=True)
            parts.append((source, peak, total))
            top = jnp.maximum(top, peak)
        weight = jnp.exp2((own_max[head] - top) * factor)
        above = own_out[head] * weight
        below = own_total[head] * weight
        for source, peak, total in parts:
            weight = jnp.exp2((peak - top) * factor)
            above = above + got_buf[source, pl.ds(0, owner_rows), :] * weight
            below = below + total * weight
        out_ref[head] = (above / below).astype(out_ref.dtype)
        return carry

    lax.fori_loop(0, KEY_VALUE_HEADS, merge, 0)

    sent = query_buf.at[pl.ds(0, n - 1)]
    pltpu.make_async_copy(sent, sent, query_send).wait()
    sent = send_buf.at[pl.ds(0, n - 1)]
    pltpu.make_async_copy(sent, sent, part_send).wait()
    for copy in pairs.values():
        copy.wait_send()


def body(
    queries,
    step_keys,
    step_values,
    sample_keys,
    sample_values,
    suffix_len,
    prompt_id,
    document_keys,
    document_values,
):
    n = lax.axis_size("seq")
    samples, steps = queries.shape[:2]
    cache = sample_keys.shape[1]
    width = KEY_VALUE_HEADS * HEAD_SIZE
    prompts, block = document_keys.shape[:2]
    group = QUERY_HEADS // KEY_VALUE_HEADS
    rows = steps * group
    owner_rows = samples * rows
    total_rows = n * owner_rows
    padded = cache + 128
    by_head = queries.reshape(samples, steps, KEY_VALUE_HEADS, group, HEAD_SIZE)
    by_head = by_head.transpose(2, 0, 1, 3, 4).reshape(KEY_VALUE_HEADS, samples, rows, HEAD_SIZE)
    marks = jnp.broadcast_to(
        prompt_id.astype(jnp.bfloat16)[None, :, None, None],
        (KEY_VALUE_HEADS, samples, ID_ROWS, HEAD_SIZE),
    )
    messages = jnp.concatenate([by_head, marks], axis=2)
    f32, bf16 = jnp.float32, jnp.bfloat16
    vmem = pl.BlockSpec(memory_space=pltpu.VMEM)
    hbm = pl.BlockSpec(memory_space=pl.ANY)
    dma = pltpu.SemaphoreType.DMA
    result = pl.pallas_call(
        functools.partial(kernel, n),
        out_shape=jax.ShapeDtypeStruct((KEY_VALUE_HEADS, owner_rows, HEAD_SIZE), bf16),
        in_specs=[pl.BlockSpec(memory_space=pltpu.SMEM), vmem, vmem, vmem, hbm, hbm, hbm, hbm],
        out_specs=vmem,
        scratch_shapes=[
            pltpu.VMEM((samples, padded, width), bf16),
            pltpu.VMEM((samples, padded, width), bf16),
            pltpu.VMEM((KEY_VALUE_HEADS, prompts, block, HEAD_SIZE), bf16),
            pltpu.VMEM((KEY_VALUE_HEADS, prompts, block, HEAD_SIZE), bf16),
            pltpu.VMEM((n, samples, rows + ID_ROWS, HEAD_SIZE), bf16),
            pltpu.VMEM((total_rows, prompts * HEAD_SIZE), bf16),
            pltpu.VMEM((total_rows, HEAD_SIZE), f32),
            pltpu.VMEM((total_rows, HEAD_SIZE), f32),
            pltpu.VMEM((total_rows, 1), f32),
            pltpu.VMEM((total_rows, 1), f32),
            pltpu.VMEM((n, owner_rows + STAT_ROWS, HEAD_SIZE), f32),
            pltpu.VMEM((n, owner_rows + STAT_ROWS, HEAD_SIZE), f32),
            pltpu.VMEM((KEY_VALUE_HEADS, owner_rows, HEAD_SIZE), f32),
            pltpu.VMEM((KEY_VALUE_HEADS, owner_rows, 1), f32),
            pltpu.VMEM((KEY_VALUE_HEADS, owner_rows, 1), f32),
            dma((4,)),
            dma,
            dma,
            dma((2, KEY_VALUE_HEADS)),
            dma((2, KEY_VALUE_HEADS)),
            dma,
            dma,
        ],
        compiler_params=pltpu.CompilerParams(
            collective_id=0, has_side_effects=True, vmem_limit_bytes=60 << 20
        ),
    )(
        suffix_len,
        messages,
        step_keys,
        step_values,
        sample_keys,
        sample_values,
        document_keys,
        document_values,
    )
    result = result.reshape(KEY_VALUE_HEADS, samples, steps, group, HEAD_SIZE)
    return result.transpose(1, 2, 0, 3, 4).reshape(samples, steps, QUERY_HEADS * HEAD_SIZE)


def solution(mesh):
    return jax.shard_map(
        body,
        mesh=mesh,
        in_specs=(
            P(("groups", "seq"), None, None),
            P(("groups", "seq"), None, None),
            P(("groups", "seq"), None, None),
            P(("groups", "seq"), None, None),
            P(("groups", "seq"), None, None),
            P(("groups", "seq")),
            P(("groups", "seq")),
            P("groups", "seq", None),
            P("groups", "seq", None),
        ),
        out_specs=P(("groups", "seq"), None, None),
        check_vma=False,
    )
```

time: 161 us -> 69.9 us (0.43)
  the two profiles are of different devices: /device:TPU:0 before, /device:TPU:29 now
where the time goes in v1:
time: 69.9 us; the launch traced here: 69.7 us
  Pallas kernels  65.6 us (94%)
  local copies, waits for them, and re-layouts  2.78 us (4%)
  other arithmetic  1.34 us (2%)
    pallas_call x1, Pallas kernels, body(): pl.pallas_call(functools.partial(kernel, n), out_shape=jax.ShapeDtypeStru...  65.6 us

profile of v1, /device:TPU:29, one launch (start us, length us, event | category | flops | bytes accessed | tf_op | source)
XLA Modules:
  0.0 69.7 jit_solution(14906270325281477198)
XLA Ops:
  0.0 0.7 convert_element_type.3
  0.7 0.1 broadcast_in_dim.2
  0.7 1.1 %reshape.13 = bf16[2,4,8,8,128]{4,3,2,1,0:T(8,128)(2,1)S(1)} reshape(bf16[2,4,8192]{2,1,0:T(4,128)(2,1)} %param.9) | data formatting | bytes 262144 | tf_op jit(solution)/shard_map/reshape | solution.py:330
  1.8 0.7 pad_maximum_fusion.query_ref
  2.5 65.6 %shard_map.91 = bf16[8,64,128]{2,1,0:T(8,128)(2,1)} custom-call(s32[2]{0:T(128)} %len_ref.1, bf16[8,2,48,128]{3,2,1,0:T(8,128)(2,1)} %pad_maximum_fusion.query_ref, bf16[2,4,1024]{2,1,0:T(4,128)(2,1)} %step_key_ref.1, bf16[2,4,1024]{2,1,0:T(4,128)(2,1)} %step_value_ref.1, bf16[2,1024,1024]{2,1,0:T(8,128)(2,1)} %sample_keys.1, ...), custom_call_target="tpu_custom_call" | custom-call | tf_op jit(solution)/shard_map/pallas_call | solution.py:341
  68.1 0.9 %copy.11 = bf16[2,4,8,8,128]{4,3,2,1,0:T(8,128)(2,1)S(1)} copy(bf16[2,4,8,8,128]{4,3,1,0,2:T(8,128)(2,1)} %bitcast.10) | data formatting | bytes 262144 | tf_op jit(solution)/shard_map/transpose | solution.py:384
  69.0 0.7 reshape.16
  (1 shorter events, 0.0 us)

commit v2 on v1

--- a/solution.py
+++ b/solution.py
@@ -117,7 +117,7 @@
     lax.fori_loop(1, n, send_query, 0)
 
     pairs = {}
-    for offset in (6, 7, 4, 5, 2, 3, 1):
+    for offset in (2, 4, 3, 5, 6, 7, 1):
         head = member(my_head, offset)
         for kind, (source, target) in enumerate(
             ((document_keys, head_keys), (document_values, head_values))
@@ -246,7 +246,10 @@
     )
     stat_row = lax.broadcasted_iota(jnp.int32, (STAT_ROWS, HEAD_SIZE), 0)
 
-    def finish(index, carry):
+    chunks = n // owners
+
+    def finish(step, carry):
+        index = lax.rem(me // owners + chunks // 2 + step, chunks)
         _, merged, top, total = attend(last, index)
         for j in range(owners):
             owner = index * owners + j

time: 69.9 us -> 60.4 us (0.86)
  the two profiles are of different devices: /device:TPU:29 before, /device:TPU:0 now
where the time goes in v2:
time: 60.4 us; the launch traced here: 60.1 us
  Pallas kernels  56 us (93%)
  local copies, waits for them, and re-layouts  2.78 us (5%)
  other arithmetic  1.34 us (2%)
    pallas_call x1, Pallas kernels, body(): pl.pallas_call(functools.partial(kernel, n), out_shape=jax.ShapeDtypeStru...  56 us

profile of v2, /device:TPU:0, one launch (start us, length us, event | category | flops | bytes accessed | tf_op | source)
XLA Modules:
  0.0 60.1 jit_solution(5924288328499319482)
XLA Ops:
  0.0 0.7 %convert_element_type.3 = bf16[2]{0:T(256)(128)(2,1)S(1)} convert(s32[2]{0:T(128)} %param.15) | non-fusion elementwise | flops 2 | bytes 12 | tf_op jit(solution)/shard_map/convert_element_type | solution.py:336
  0.7 0.1 broadcast_in_dim.2
  0.7 1.1 %reshape.13 = bf16[2,4,8,8,128]{4,3,2,1,0:T(8,128)(2,1)S(1)} reshape(bf16[2,4,8192]{2,1,0:T(4,128)(2,1)} %param.9) | data formatting | bytes 262144 | tf_op jit(solution)/shard_map/reshape | solution.py:333
  1.8 0.7 %pad_maximum_fusion.query_ref = bf16[8,2,48,128]{3,2,1,0:T(8,128)(2,1)} fusion(bf16[8,2,16,128]{3,2,1,0:T(8,128)(2,1)S(1)} %broadcast_in_dim.2, bf16[8,2,32,128]{3,2,1,0:T(8,128)(2,1)S(1)} %bitcast.11), kind=kLoop, calls=%fused_computation | loop fusion | flops 393216 | bytes 393216 | tf_op jit(solution)/shard_map/concatenate | solution.py:339
  2.5 56.0 %shard_map.91 = bf16[8,64,128]{2,1,0:T(8,128)(2,1)} custom-call(s32[2]{0:T(128)} %len_ref.1, bf16[8,2,48,128]{3,2,1,0:T(8,128)(2,1)} %pad_maximum_fusion.query_ref, bf16[2,4,1024]{2,1,0:T(4,128)(2,1)} %step_key_ref.1, bf16[2,4,1024]{2,1,0:T(4,128)(2,1)} %step_value_ref.1, bf16[2,1024,1024]{2,1,0:T(8,128)(2,1)} %sample_keys.1, ...), custom_call_target="tpu_custom_call" | custom-call | tf_op jit(solution)/shard_map/pallas_call | solution.py:344
  58.5 0.9 %copy.11 = bf16[2,4,8,8,128]{4,3,2,1,0:T(8,128)(2,1)S(1)} copy(bf16[2,4,8,8,128]{4,3,1,0,2:T(8,128)(2,1)} %bitcast.10) | data formatting | bytes 262144 | tf_op jit(solution)/shard_map/transpose | solution.py:387
  59.4 0.7 %reshape.16 = bf16[2,4,8192]{2,1,0:T(4,128)(2,1)} reshape(bf16[2,4,8,8,128]{4,3,2,1,0:T(8,128)(2,1)S(1)} %copy.11) | data formatting | bytes 262144 | tf_op jit(solution)/shard_map/reshape | solution.py:387
  (1 shorter events, 0.0 us)
